TPU v7x, 32 devices: a whole 2x2x4 slice. The times are simulated.
32 devices in a mesh: dp: 8 (over z, core), expert: 4 (over y, x).
Axes of the slice: x: 2, y: 2, z: 4, core: 2. Of those that a mesh axis runs over, the one named last changes fastest.
Arguments:
- tokens: bfloat16 [24576, 2048], P(('dp', 'expert')), may hold values from -6 to 6
- target: bfloat16 [24576, 2048], P(('dp', 'expert')), may hold values from -4 to 4
- route_index: int32 [8, 4, 4, 16], P('dp', None, 'expert'), may hold values from 0 to 767, as said below
- route_count: int32 [8, 4, 4], P('dp', None, 'expert'), may hold values from 1 to 16, as said below
- route_gate: float32 [8, 4, 4, 16], P('dp', None, 'expert'), may hold values from 0.1 to 1
- gate_weight: bfloat16 [2048, 4, 768], P('dp', 'expert'), may hold values from -0.125 to 0.125
- up_weight: bfloat16 [2048, 4, 768], P('dp', 'expert'), may hold values from -0.125 to 0.125
- down_weight: bfloat16 [2048, 4, 768], P('dp', 'expert'), may hold values from -0.21875 to 0.21875
Outputs:
- token_grad: bfloat16 [24576, 2048], P(('dp', 'expert'))
- gate_gradient: float32 [2048, 4, 768], P('dp', 'expert')
- up_gradient: float32 [2048, 4, 768], P('dp', 'expert')
- down_gradient: float32 [2048, 4, 768], P('dp', 'expert')
Inputs may be any that keep to these rules, and one draw needn't show every extreme that they name: `route_index`: within each list of 16 slots the indices are distinct; each names a token of the source device. `route_count`: in every group one expert has all 16 slots live from every source device; slots at or beyond the count are unused.
All inputs are finite; a program needn't handle non-finite values.
Results may differ from a plain program's by a relative error of at most 0.0059.
Values may be sent and summed in bfloat16 or wider, within the bound.
A program may use at most 128 MiB of HBM per device.

v0:
```python
import jax
import jax.numpy as jnp
from jax import lax
from jax.sharding import PartitionSpec as P


def to_owners(block):
    return lax.all_to_all(block, "expert", split_axis=0, concat_axis=1, tiled=True)


def to_sources(block):
    return lax.all_to_all(block, "expert", split_axis=1, concat_axis=0, tiled=True)


def on_device(
    tokens, target, route_index, route_count, route_gate, gate_weight, up_weight, down_weight
):
    groups = lax.axis_size("dp")
    sources = lax.axis_size("expert")
    local_index = route_index[0, :, 0, :]
    live_count = route_count[0, :, 0]
    per_source = local_index.shape[1]
    model_width = tokens.shape[1]
    usable = jnp.arange(per_source, dtype=jnp.int32)[None, :] < live_count[:, None]
    slot_weight = jnp.where(usable, route_gate[0, :, 0, :], 0.0)
    outgoing = tokens[local_index] * usable[:, :, None].astype(tokens.dtype)
    expert_rows = to_owners(outgoing)
    full_gate, full_up, full_down = (
        lax.all_gather(gate_weight, "dp", axis=0, tiled=True),
        lax.all_gather(up_weight, "dp", axis=0, tiled=True),
        lax.all_gather(down_weight, "dp", axis=0, tiled=True),
    )
    gate_pre = jnp.einsum(
        "erd,def->erf", expert_rows, full_gate, preferred_element_type=jnp.float32
    )
    up_pre = jnp.einsum("erd,def->erf", expert_rows, full_up, preferred_element_type=jnp.float32)
    sigma = jax.nn.sigmoid(gate_pre)
    active = gate_pre * sigma
    hidden = (active * up_pre).astype(jnp.bfloat16)
    expert_out = jnp.einsum(
        "erf,def->erd", hidden, full_down, preferred_element_type=jnp.float32
    ).astype(jnp.bfloat16)
    returned = to_sources(expert_out)
    flat_index = local_index.reshape(-1)
    combined = (
        jnp.zeros((tokens.shape[0], model_width), jnp.float32)
        .at[flat_index]
        .add((slot_weight[:, :, None] * returned.astype(jnp.float32)).reshape(-1, model_width))
    )
    out_grad = combined - target.astype(jnp.float32)
    slot_grad = (slot_weight[:, :, None] * out_grad[local_index]).astype(jnp.bfloat16)
    owner_grad = to_owners(slot_grad)
    hidden_grad = jnp.einsum(
        "erd,def->erf", owner_grad, full_down, preferred_element_type=jnp.float32
    )
    gate_grad = (hidden_grad * up_pre * sigma * (1.0 + gate_pre * (1.0 - sigma))).astype(
        jnp.bfloat16
    )
    up_grad = (hidden_grad * active).astype(jnp.bfloat16)
    row_grad = (
        jnp.einsum("erf,def->erd", gate_grad, full_gate, preferred_element_type=jnp.float32)
        + jnp.einsum("erf,def->erd", up_grad, full_up, preferred_element_type=jnp.float32)
    ).astype(jnp.bfloat16)
    came_back = to_sources(row_grad)
    token_grad = (
        jnp.zeros((tokens.shape[0], model_width), jnp.float32)
        .at[flat_index]
        .add(came_back.astype(jnp.float32).reshape(-1, model_width))
        .astype(jnp.bfloat16)
    )
    factor = (groups * sources * per_source) ** (-0.5)
    rows_every, grad_every = (
        lax.all_to_all(expert_rows, "dp", split_axis=2, concat_axis=1, tiled=True),
        lax.all_to_all(owner_grad, "dp", split_axis=2, concat_axis=1, tiled=True),
    )
    hidden_piece = lax.all_gather(hidden, "dp", axis=1, tiled=True)
    gate_piece = lax.all_gather(gate_grad, "dp", axis=1, tiled=True)
    up_piece = lax.all_gather(up_grad, "dp", axis=1, tiled=True)
    gate_sum = jnp.einsum(
        "erd,erf->def", rows_every, gate_piece, preferred_element_type=jnp.float32
    )
    up_sum = jnp.einsum("erd,erf->def", rows_every, up_piece, preferred_element_type=jnp.float32)
    down_sum = jnp.einsum(
        "erd,erf->def", grad_every, hidden_piece, preferred_element_type=jnp.float32
    )
    gate_gradient = gate_sum * factor
    up_gradient = up_sum * factor
    down_gradient = down_sum * factor
    return (token_grad, gate_gradient, up_gradient, down_gradient)


def solution(mesh):
    return jax.shard_map(
        on_device,
        mesh=mesh,
        in_specs=(
            P(("dp", "expert"), None),
            P(("dp", "expert"), None),
            P("dp", None, "expert", None),
            P("dp", None, "expert"),
            P("dp", None, "expert", None),
            P("dp", "expert", None),
            P("dp", "expert", None),
            P("dp", "expert", None),
        ),
        out_specs=(
            P(("dp", "expert"), None),
            P("dp", "expert", None),
            P("dp", "expert", None),
            P("dp", "expert", None),
        ),
        check_vma=False,
    )
```

profile of v0, /device:TPU:0, one launch (start us, length us, event | category | flops | bytes accessed | tf_op | source)
XLA Modules:
  0.0 305.2 jit_solution(9919206521907058066)
XLA Ops:
  11.8 5.2 %all-to-all-start = ((bf16[4,16,2048]{2,1,0:T(8,128)(2,1)}), bf16[4,16,2048]{2,1,0:T(8,128)(2,1)S(1)}, u32[]{:S(2)}, u32[]{:S(2)}) async-start(bf16[4,16,2048]{2,1,0:T(8,128)(2,1)} %broadcast_multiply_fusion), calls=%async_computation | async-start | bytes 524288 | tf_op jit(solution)/shard_map/all_to_all | solution.py:8
  18.3 4.1 %all-to-all-done = bf16[4,16,2048]{2,1,0:T(8,128)(2,1)S(1)} async-done(((bf16[4,16,2048]{2,1,0:T(8,128)(2,1)}), bf16[4,16,2048]{2,1,0:T(8,128)(2,1)S(1)}, u32[]{:S(2)}, u32[]{:S(2)}) %all-to-all-start) | async-done | bytes 262176 | tf_op jit(solution)/shard_map/all_to_all | solution.py:8
  22.4 1.9 copy.40
  24.9 13.3 %reduce.10 = bf16[2048,64]{1,0:T(8,128)(2,1)} reduce(bf16[2048,1,64]{2,1,0:T(2,128)(2,1)} %bitcast.114, bf16[]{:T(256)} %broadcast.134), dimensions={1}, to_apply=%bitcast.86.reduce_sub_computation | reduce | bytes 524290
  38.2 2.1 reshape.301
  40.3 4.9 %all-to-all-start.4 = ((bf16[8,2,8192]{2,1,0:T(2,128)(2,1)}), bf16[8,2,8192]{2,1,0:T(2,128)(2,1)}, u32[]{:S(2)}, u32[]{:S(2)}) async-start(bf16[8,2,8192]{2,1,0:T(2,128)(2,1)} %reshape.301), calls=%async_computation.4 | async-start | bytes 524288 | tf_op jit(solution)/shard_map/all_to_all | solution.py:73
  46.6 8.4 %all-to-all-done.4 = bf16[8,2,8192]{2,1,0:T(2,128)(2,1)} async-done(((bf16[8,2,8192]{2,1,0:T(2,128)(2,1)}), bf16[8,2,8192]{2,1,0:T(2,128)(2,1)}, u32[]{:S(2)}, u32[]{:S(2)}) %all-to-all-start.4) | async-done | bytes 262176 | tf_op jit(solution)/shard_map/all_to_all | solution.py:73
  55.0 3.4 %reshape.302 = bf16[2048,1,64]{2,1,0:T(2,128)(2,1)} reshape(bf16[8,2,8192]{2,1,0:T(2,128)(2,1)} %all-to-all-done.4) | data formatting | bytes 524288
  58.4 3.4 %copy.41 = bf16[1,64,2048]{2,1,0:T(8,128)(2,1)} copy(bf16[1,64,2048]{1,0,2:T(2,128)(2,1)} %bitcast.112) | data formatting | bytes 524288 | tf_op jit(solution)/shard_map/all_to_all | solution.py:73
  61.8 1.7 copy.49
  63.5 3.2 %fusion.10 = f32[64,768]{1,0:T(8,128)} fusion(bf16[64,2048]{1,0:T(8,128)(2,1)S(1)} %bitcast.117, bf16[2048,1,768]{2,0,1:T(8,128)(2,1)} %all-gather.7.cloned.1.call-done), kind=kOutput, calls=%fused_computation.15 | convolution fusion | flops 201326592 | bytes 3604480 | tf_op jit(solution)/shard_map/erd,def->erf/dot_general | solution.py:33
  66.8 24.2 %all-gather.9.cloned.1.call-done = bf16[2048,1,768]{2,0,1:T(8,128)(2,1)} async-done(((bf16[256,1,768]{2,0,1:T(8,128)(2,1)}), bf16[2048,1,768]{2,0,1:T(8,128)(2,1)}) %all-gather.9.cloned.1.call-update) | async-done | bytes 3145744 | tf_op jit(solution)/shard_map/all_gather | solution.py:30
  90.9 3.2 %multiply_convert_fusion.3 = (bf16[64,768]{1,0:T(8,128)(2,1)S(1)}, f32[64,768]{1,0:T(8,128)}) fusion(f32[64,768]{1,0:T(8,128)} %fusion.10, bf16[64,2048]{1,0:T(8,128)(2,1)S(1)} %bitcast.118, bf16[2048,1,768]{2,0,1:T(8,128)(2,1)} %all-gather.9.cloned.1.call-done), kind=kOutput, calls=%fused_computation.44 | convolution fusion | flops 201621504 | bytes 3899392 | tf_op jit(solution)/shard_map/erd,def->erf/dot_general | solution.py:36
  94.1 35.6 %all-gather.11.cloned.1.call-done = bf16[2048,1,768]{2,0,1:T(8,128)(2,1)} async-done(((bf16[256,1,768]{2,0,1:T(8,128)(2,1)}), bf16[2048,1,768]{2,0,1:T(8,128)(2,1)}) %all-gather.11.cloned.1.call-update) | async-done | bytes 3145744 | tf_op jit(solution)/shard_map/all_gather | solution.py:31
  129.7 3.0 fusion.25
  132.7 1.2 copy.62
  133.9 3.8 %reduce.8 = bf16[64,2048]{1,0:T(8,128)(2,1)} reduce(bf16[64,1,2048]{2,1,0:T(2,128)(2,1)} %bitcast.123, bf16[]{:T(256)} %broadcast.134), dimensions={1}, to_apply=%bitcast.109.reduce_sub_computation | reduce | bytes 524290
  137.7 1.8 reshape.297
  139.5 4.2 %all-to-all-start.1 = ((bf16[4,2,16384]{2,1,0:T(2,128)(2,1)}), bf16[4,2,16384]{2,1,0:T(2,128)(2,1)}, u32[]{:S(2)}, u32[]{:S(2)}) async-start(bf16[4,2,16384]{2,1,0:T(2,128)(2,1)} %reshape.297), calls=%async_computation.1 | async-start | bytes 524288 | tf_op jit(solution)/shard_map/all_to_all | solution.py:12
  143.8 5.8 %all-to-all-done.1 = bf16[4,2,16384]{2,1,0:T(2,128)(2,1)} async-done(((bf16[4,2,16384]{2,1,0:T(2,128)(2,1)}), bf16[4,2,16384]{2,1,0:T(2,128)(2,1)}, u32[]{:S(2)}, u32[]{:S(2)}) %all-to-all-start.1) | async-done | bytes 262176 | tf_op jit(solution)/shard_map/all_to_all | solution.py:12
  149.7 1.9 reshape.298
  151.5 5.1 %scatter_custom_fusion = f32[768,2048]{1,0:T(8,128)} fusion(s32[64]{0:T(128)S(1)} %fusion.41, f32[]{:T(128)} %constant.5.clone.1, bf16[1,64,2048]{2,0,1:T(2,128)(2,1)} %bitcast.122, f32[64]{0:T(128)S(1)} %broadcast_select_fusion.1), kind=kCustom, calls=%fused_computation.19 | custom fusion | flops 393216 | bytes 6554116 | tf_op jit(solution)/shard_map/scatter-add | solution.py:48
  156.6 7.9 %convert_subtract_fusion = f32[768,2048]{1,0:T(8,128)} fusion(f32[768,2048]{1,0:T(8,128)} %scatter_custom_fusion, bf16[768,2048]{1,0:T(8,128)(2,1)} %param.9), kind=kLoop, calls=%fused_computation.4 | loop fusion | flops 3145728 | bytes 15728640 | tf_op jit(solution)/shard_map/sub | solution.py:50
  164.4 4.6 %gather_fusion.1 = f32[64,2048]{1,0:T(8,128)} fusion(f32[768,2048]{1,0:T(8,128)} %convert_subtract_fusion, s32[1024]{0:T(1024)S(1)} %pad_clamp_fusion), kind=kCustom, calls=%fused_computation.1 | custom fusion | bytes 1048832 | tf_op jit(solution)/shard_map/gather | solution.py:51
  169.0 1.8 multiply_convert_fusion
  170.8 4.1 %all-to-all-start.2 = ((bf16[4,16,2048]{2,1,0:T(8,128)(2,1)}), bf16[4,16,2048]{2,1,0:T(8,128)(2,1)}, u32[]{:S(2)}, u32[]{:S(2)}) async-start(bf16[4,16,2048]{2,1,0:T(8,128)(2,1)} %multiply_convert_fusion), calls=%async_computation.2 | async-start | bytes 524288 | tf_op jit(solution)/shard_map/all_to_all | solution.py:8
  174.9 16.5 %all-gather.2 = bf16[512,768]{1,0:T(8,128)(2,1)} all-gather(bf16[64,768]{1,0:T(8,128)(2,1)S(1)} %get-tuple-element.28), channel_id=4, replica_groups=mesh['dp'=8,'expert'=4] {'dp'}, dimensions={0}, use_global_device_ids=true | all-gather | bytes 884736 | tf_op jit(solution)/shard_map/all_gather | solution.py:76
  191.4 2.8 multiply_convert_fusion.2
  197.7 3.8 %reduce.9 = bf16[64,2048]{1,0:T(8,128)(2,1)} reduce(bf16[64,1,2048]{2,1,0:T(2,128)(2,1)} %bitcast.124, bf16[]{:T(256)} %broadcast.134), dimensions={1}, to_apply=%bitcast.108.reduce_sub_computation | reduce | bytes 524290
  201.5 1.9 reshape.299
  203.4 4.2 %all-to-all-start.3 = ((bf16[4,2,16384]{2,1,0:T(2,128)(2,1)}), bf16[4,2,16384]{2,1,0:T(2,128)(2,1)}, u32[]{:S(2)}, u32[]{:S(2)}) async-start(bf16[4,2,16384]{2,1,0:T(2,128)(2,1)} %reshape.299), calls=%async_computation.3 | async-start | bytes 524288 | tf_op jit(solution)/shard_map/all_to_all | solution.py:12
  207.6 16.5 %all-gather = bf16[512,768]{1,0:T(8,128)(2,1)S(1)} all-gather(bf16[64,768]{1,0:T(8,128)(2,1)} %copy-done.4), channel_id=2, replica_groups=mesh['dp'=8,'expert'=4] {'dp'}, dimensions={0}, use_global_device_ids=true | all-gather | bytes 884736 | tf_op jit(solution)/shard_map/all_gather | solution.py:77
  224.1 1.3 fusion.33
  225.4 3.0 copy.46
  228.4 3.4 %copy.43 = bf16[1,64,2048]{1,0,2:T(2,128)(2,1)} copy(bf16[1,64,2048]{2,1,0:T(8,128)(2,1)} %bitcast.22) | data formatting | bytes 524288 | tf_op jit(solution)/shard_map/all_to_all | solution.py:8
  231.8 13.3 %reduce.11 = bf16[2048,64]{1,0:T(8,128)(2,1)} reduce(bf16[2048,1,64]{2,1,0:T(2,128)(2,1)} %bitcast.115, bf16[]{:T(256)} %broadcast.134), dimensions={1}, to_apply=%bitcast.88.reduce_sub_computation | reduce | bytes 524290
  245.1 2.1 reshape.303
  247.3 4.1 %all-to-all-start.5 = ((bf16[8,2,8192]{2,1,0:T(2,128)(2,1)}), bf16[8,2,8192]{2,1,0:T(2,128)(2,1)}, u32[]{:S(2)}, u32[]{:S(2)}) async-start(bf16[8,2,8192]{2,1,0:T(2,128)(2,1)} %reshape.303), calls=%async_computation.5 | async-start | bytes 524288 | tf_op jit(solution)/shard_map/all_to_all | solution.py:74
  251.3 19.9 %all-gather.1 = bf16[512,768]{1,0:T(8,128)(2,1)S(1)} all-gather(bf16[64,768]{1,0:T(8,128)(2,1)S(1)} %get-tuple-element.25), channel_id=3, replica_groups=mesh['dp'=8,'expert'=4] {'dp'}, dimensions={0}, use_global_device_ids=true | all-gather | bytes 884736 | tf_op jit(solution)/shard_map/all_gather | solution.py:78
  271.3 1.3 fusion.32
  272.6 3.0 copy.47
  275.6 1.9 reshape.300
  277.5 5.1 %scatter_custom_fusion.1 = f32[768,2048]{1,0:T(8,128)} fusion(s32[64]{0:T(128)S(1)} %fusion.41, f32[]{:T(128)} %constant.5.clone.1, bf16[1,64,2048]{2,0,1:T(2,128)(2,1)} %bitcast.125), kind=kCustom, calls=%fused_computation.17 | custom fusion | flops 262144 | bytes 6553604 | tf_op jit(solution)/shard_map/scatter-add | solution.py:68
  282.5 4.9 %convert_element_type.75 = bf16[768,2048]{1,0:T(8,128)(2,1)} convert(f32[768,2048]{1,0:T(8,128)} %scatter_custom_fusion.1) | non-fusion elementwise | flops 1572864 | bytes 9437184 | tf_op jit(solution)/shard_map/convert_element_type | solution.py:69
  287.5 3.4 %reshape.304 = bf16[2048,1,64]{2,1,0:T(2,128)(2,1)} reshape(bf16[8,2,8192]{2,1,0:T(2,128)(2,1)} %all-to-all-done.5) | data formatting | bytes 524288
  290.8 2.3 copy.44
  293.3 2.4 fusion.31
  295.7 3.0 copy.48
  (51 shorter events, 11.5 us)
Async XLA Ops:
  7.2 3.0 copy-start
  7.2 10.4 %copy-start.5 = (s32[1,4,1,16]{3,2,1,0:T(1,128)S(1)}, s32[1,4,1,16]{3,2,1,0:T(1,128)}, u32[]{:S(2)}) copy-start(s32[1,4,1,16]{3,2,1,0:T(1,128)} %param.10) | copy-start | bytes 772
  7.2 3.8 %copy-start.7 = (s32[1,4,1]{1,2,0:T(1,128)S(1)}, s32[1,4,1]{1,2,0:T(1,128)}, u32[]{:S(2)}) copy-start(s32[1,4,1]{1,2,0:T(1,128)} %param.11) | copy-start | bytes 52
  7.2 56.3 %all-gather.7.cloned.1.call-start = ((), (), s32[]{:S(2)}) async-start(), calls=%async_computation.6 | async-start | bytes 3538944 | tf_op jit(solution)/shard_map/all_gather | solution.py:29
  7.9 83.0 %all-gather.9.cloned.1.call-start = ((), (), s32[]{:S(2)}) async-start(), calls=%async_computation.7 | async-start | bytes 3538944 | tf_op jit(solution)/shard_map/all_gather | solution.py:30
  8.7 121.0 %all-gather.11.cloned.1.call-start = ((), (), s32[]{:S(2)}) async-start(), calls=%async_computation.8 | async-start | bytes 3538944 | tf_op jit(solution)/shard_map/all_gather | solution.py:31
  10.9 34.9 %copy-start.6 = (f32[1,4,1,16]{3,2,1,0:T(1,128)S(1)}, f32[1,4,1,16]{3,2,1,0:T(1,128)}, u32[]{:S(2)}) copy-start(f32[1,4,1,16]{3,2,1,0:T(1,128)} %param.12) | copy-start | bytes 772
  11.8 10.6 %all-to-all-start = ((bf16[4,16,2048]{2,1,0:T(8,128)(2,1)}), bf16[4,16,2048]{2,1,0:T(8,128)(2,1)S(1)}, u32[]{:S(2)}, u32[]{:S(2)}) async-start(bf16[4,16,2048]{2,1,0:T(8,128)(2,1)} %broadcast_multiply_fusion), calls=%async_computation | async-start | bytes 524288 | tf_op jit(solution)/shard_map/all_to_all | solution.py:8
  40.3 14.7 %all-to-all-start.4 = ((bf16[8,2,8192]{2,1,0:T(2,128)(2,1)}), bf16[8,2,8192]{2,1,0:T(2,128)(2,1)}, u32[]{:S(2)}, u32[]{:S(2)}) async-start(bf16[8,2,8192]{2,1,0:T(2,128)(2,1)} %reshape.301), calls=%async_computation.4 | async-start | bytes 524288 | tf_op jit(solution)/shard_map/all_to_all | solution.py:73
  94.1 49.6 %copy-start.3 = (bf16[8,8,8,256]{3,2,1,0:T(8,128)(2,1)S(1)}, bf16[8,8,8,256]{3,2,1,0:T(8,128)(2,1)}, u32[]{:S(2)}) copy-start(bf16[8,8,8,256]{3,2,1,0:T(8,128)(2,1)} %copy.49) | copy-start | bytes 786436
  139.5 10.2 %all-to-all-start.1 = ((bf16[4,2,16384]{2,1,0:T(2,128)(2,1)}), bf16[4,2,16384]{2,1,0:T(2,128)(2,1)}, u32[]{:S(2)}, u32[]{:S(2)}) async-start(bf16[4,2,16384]{2,1,0:T(2,128)(2,1)} %reshape.297), calls=%async_computation.1 | async-start | bytes 524288 | tf_op jit(solution)/shard_map/all_to_all | solution.py:12
  170.8 20.5 %all-to-all-start.2 = ((bf16[4,16,2048]{2,1,0:T(8,128)(2,1)}), bf16[4,16,2048]{2,1,0:T(8,128)(2,1)}, u32[]{:S(2)}, u32[]{:S(2)}) async-start(bf16[4,16,2048]{2,1,0:T(8,128)(2,1)} %multiply_convert_fusion), calls=%async_computation.2 | async-start | bytes 524288 | tf_op jit(solution)/shard_map/all_to_all | solution.py:8
  191.4 3.0 copy-start.2
  191.4 4.1 %copy-start.1 = (bf16[2048,1,768]{2,0,1:T(8,128)(2,1)S(1)}, bf16[2048,1,768]{2,0,1:T(8,128)(2,1)}, u32[]{:S(2)}) copy-start(bf16[2048,1,768]{2,0,1:T(8,128)(2,1)} %all-gather.7.cloned.1.call-done) | copy-start | bytes 9437188
  194.2 2.3 copy-start.4
  203.4 43.9 %all-to-all-start.3 = ((bf16[4,2,16384]{2,1,0:T(2,128)(2,1)}), bf16[4,2,16384]{2,1,0:T(2,128)(2,1)}, u32[]{:S(2)}, u32[]{:S(2)}) async-start(bf16[4,2,16384]{2,1,0:T(2,128)(2,1)} %reshape.299), calls=%async_computation.3 | async-start | bytes 524288 | tf_op jit(solution)/shard_map/all_to_all | solution.py:12
  247.3 40.2 %all-to-all-start.5 = ((bf16[8,2,8192]{2,1,0:T(2,128)(2,1)}), bf16[8,2,8192]{2,1,0:T(2,128)(2,1)}, u32[]{:S(2)}, u32[]{:S(2)}) async-start(bf16[8,2,8192]{2,1,0:T(2,128)(2,1)} %reshape.303), calls=%async_computation.5 | async-start | bytes 524288 | tf_op jit(solution)/shard_map/all_to_all | solution.py:74
Sparse Core Ops, SparseCore 0:
  9.6 40.9 all-gather.6
  52.3 38.6 all-gather.8
  92.6 37.1 all-gather.10
where the time goes:
time: 307 us; the launch traced here: 305 us
  waiting for transfers between devices  80.1 us (26%)
  other arithmetic  62 us (20%)
  blocking collectives  52.9 us (17%)
  local copies, waits for them, and re-layouts  50.3 us (16%)
  starting transfers between devices  26.7 us (9%)
  matrix products  19.3 us (6%)
  between operations  13.9 us (5%)
    all_gather x1, waiting for transfers between devices, on_device(): lax.all_gather(down_weight, 'dp', axis=0, tiled=True)  35.6 us
    unnamed x6, other arithmetic  35.6 us
    unnamed x32, local copies, waits for them, and re-layouts  31.1 us
    all_gather x1, waiting for transfers between devices, on_device(): lax.all_gather(up_weight, 'dp', axis=0, tiled=True)  24.2 us
    all_gather x1, blocking collectives, on_device(): up_piece = lax.all_gather(up_grad, 'dp', axis=1, tiled=True)  19.9 us
    all_gather x1, blocking collectives, on_device(): gate_piece = lax.all_gather(gate_grad, 'dp', axis=1, tiled=True)  16.5 us
    all_gather x1, blocking collectives, on_device(): hidden_piece = lax.all_gather(hidden, 'dp', axis=1, tiled=True)  16.5 us
    all_to_all x2, starting transfers between devices, to_owners(): lax.all_to_all(block, 'expert', split_axis=0, concat_axis=1, tiled=True)  9.24 us
  transfers between devices with their start and end apart: 9, of which 5 were waited for; matrix products, arithmetic and copies ran while one was open for 25% of the time, Pallas kernels for 0%

commit v1 on v0

v1 whole, which is shorter than its diff:
```python
import functools

import jax
import jax.numpy as jnp
from jax import lax
from jax.experimental import pallas as pl
from jax.experimental.pallas import tpu as pltpu
from jax.sharding import PartitionSpec as P

F32 = jnp.float32
BF16 = jnp.bfloat16
CORES = 2


def dot(a, b, dims, precision=None):
    return lax.dot_general(
        a, b, (dims, ((), ())), preferred_element_type=F32, precision=precision
    )


NN = ((1,), (0,))
NT = ((1,), (1,))
TN = ((0,), (0,))


def kernel(
    planes, experts, slots, factor,
    rows, tgt, amat, wcol, gw, uw, dw,
    cb_out, gg_out, ug_out, dg_out,
    W, R, EO, RET, SG, G, RG, CB, PS, PR, HS, HR, H, GU, RX, GX, HX, GUX,
    w_loc, w_send, w_recv, a_loc, a_send, a_recv, p_send, p_recv,
    h_send, h_recv, x_send, x_recv,
):
    dp = lax.axis_index("dp")
    me_e = lax.axis_index("expert")
    me_z = dp // CORES
    core = dp % CORES
    peers = planes * experts
    per_group = experts * slots
    all_rows = planes * per_group
    half = gw.shape[0]
    chunk = CORES * half
    ff = gw.shape[1]
    me = me_z * experts + me_e
    sibling = {"dp": me_z * CORES + (1 - core), "expert": me_e}

    def at(z, e):
        return {"dp": z * CORES + core, "expert": e}

    barrier = pltpu.get_barrier_semaphore()

    def greet(k, carry):
        p = (me + k) % peers
        pl.semaphore_signal(
            barrier, inc=1, device_id=at(p // experts, p % experts),
            device_id_type=pl.DeviceIdType.MESH,
        )
        return carry

    lax.fori_loop(1, peers, greet, 0)
    pl.semaphore_signal(
        barrier, inc=1, device_id=sibling, device_id_type=pl.DeviceIdType.MESH
    )
    locals_w = []
    for i, w in enumerate((gw, uw, dw)):
        c = pltpu.make_async_copy(w, W.at[i, core], w_loc.at[i])
        c.start()
        locals_w.append(c)
    pl.semaphore_wait(barrier, peers)

    def slot_rows(n):
        return pl.ds(pl.multiple_of(n * slots, slots), slots)

    def cols(z):
        return pl.ds(pl.multiple_of(z * chunk, chunk), chunk)

    def group_rows(z):
        return pl.ds(pl.multiple_of(z * per_group, per_group), per_group)

    def remote(src, dst, s, r, dev):
        c = pltpu.make_async_remote_copy(
            src_ref=src, dst_ref=dst, send_sem=s, recv_sem=r,
            device_id=dev, device_id_type=pl.DeviceIdType.MESH,
        )
        c.start()
        return c

    def out_to_owners(src, dst, i):
        pltpu.make_async_copy(
            src.at[slot_rows(me_e), cols(me_z)], dst.at[slot_rows(me)], a_loc.at[i]
        ).start()

        def body(k, carry):
            p = (me + k) % peers
            z, e = p // experts, p % experts
            remote(
                src.at[slot_rows(e), cols(z)], dst.at[slot_rows(me)],
                a_send.at[i], a_recv.at[i], at(z, e),
            )
            return carry

        lax.fori_loop(1, peers, body, 0)

    def out_to_sources(src, dst, i):
        pltpu.make_async_copy(
            src.at[slot_rows(me)], dst.at[slot_rows(me_e), cols(me_z)], a_loc.at[i]
        ).start()

        def body(k, carry):
            p = (me + k) % peers
            z, e = p // experts, p % experts
            remote(
                src.at[slot_rows(p)], dst.at[slot_rows(me_e), cols(me_z)],
                a_send.at[i], a_recv.at[i], at(z, e),
            )
            return carry

        lax.fori_loop(1, peers, body, 0)

    def take(sem, ref):
        pltpu.make_async_copy(ref, ref, sem).wait()

    some = pl.ds(0, (peers - 1) * slots)

    def arrived(i):
        take(a_recv.at[i], R.at[some])
        take(a_loc.at[i], R.at[pl.ds(0, slots)])

    out_to_owners(rows, R, 0)
    sent_w = [
        remote(w, W.at[i, core], w_send.at[i], w_recv.at[i], sibling)
        for i, w in enumerate((gw, uw, dw))
    ]

    step = min(256, all_rows)
    steps = all_rows // step

    def row_loop(fn):
        def body(j, carry):
            fn(pl.ds(pl.multiple_of(j * step, step), step))
            return carry

        lax.fori_loop(0, steps, body, 0)

    def scatter_sums(src, dst, i):
        for k in range(planes - 1, 0, -1):
            z = (me_z + k) % planes
            remote(
                src.at[group_rows(z)], dst.at[k - 1],
                p_send.at[i], p_recv.at[i], at(z, me_e),
            )

    def gather_rows(buf, i):
        for k in range(planes - 1, 0, -1):
            z = (me_z + k) % planes
            remote(
                buf.at[group_rows(me_z)], buf.at[group_rows(me_z)],
                h_send.at[i], h_recv.at[i], at(z, me_e),
            )

    def total(part, i, src, own):
        take(p_recv.at[i], part)
        for k in range(planes - 1):
            own = own + part[k].astype(F32)
        return own

    def weight(i):
        return W[i].reshape(chunk, ff)

    keep = pl.ds(pl.multiple_of(core * half, half), half)
    give = pl.ds(pl.multiple_of((1 - core) * half, half), half)

    arrived(0)
    for i in range(2):
        locals_w[i].wait()
        sent_w[i].wait_recv()

        def partial(rs, i=i):
            PS[i, rs, :] = dot(R[rs, :], weight(i), NN).astype(BF16)

        row_loop(partial)
        scatter_sums(PS.at[i], PR.at[i], i)
    x_rows = remote(R.at[:, give], RX, x_send.at[0], x_recv.at[0], sibling)
    mine = group_rows(me_z)
    gate_own = dot(R[mine, :], weight(0), NN)
    up_own = dot(R[mine, :], weight(1), NN)
    gate_pre = total(PR.at[0], 0, PS, gate_own)
    up_pre = total(PR.at[1], 1, PS, up_own)
    sigma = jax.nn.sigmoid(gate_pre)
    active = gate_pre * sigma
    H[mine, :] = (active * up_pre).astype(BF16)
    gather_rows(H, 0)
    locals_w[2].wait()
    sent_w[2].wait_recv()
    some_groups = pl.ds(0, (planes - 1) * per_group)
    take(h_recv.at[0], H.at[some_groups])

    def expert_out(rs):
        EO[rs, :] = dot(H[rs, :], weight(2), NT).astype(BF16)

    row_loop(expert_out)
    out_to_sources(EO, RET, 1)
    x_hidden = remote(H, HX, x_send.at[1], x_recv.at[1], sibling)
    arrived(1)
    for z in range(planes):
        piece = slice(z * chunk, (z + 1) * chunk)
        combined = dot(
            amat[...], RET[:, piece].astype(F32), NN, lax.Precision.HIGHEST
        )
        SG[:, piece] = (
            wcol[...] * (combined - tgt[:, piece].astype(F32))
        ).astype(BF16)
    out_to_owners(SG, G, 2)
    arrived(2)

    def hidden_partial(rs):
        HS[rs, :] = dot(G[rs, :], weight(2), NN).astype(BF16)

    row_loop(hidden_partial)
    scatter_sums(HS, HR, 2)
    x_grad = remote(G.at[:, give], GX, x_send.at[2], x_recv.at[2], sibling)
    own = dot(G[mine, :], weight(2), NN)
    hidden_grad = total(HR, 2, HS, own)
    GU[0, mine, :] = (
        hidden_grad * up_pre * sigma * (1.0 + gate_pre * (1.0 - sigma))
    ).astype(BF16)
    gather_rows(GU.at[0], 1)
    GU[1, mine, :] = (hidden_grad * active).astype(BF16)
    gather_rows(GU.at[1], 2)
    x_hidden.wait_recv()
    x_grad.wait_recv()
    x_rows.wait_recv()
    dg_out[...] = (dot(G[:, keep], H[...], TN) + dot(GX[...], HX[...], TN)) * factor
    take(h_recv.at[1], GU.at[0, some_groups])
    x_gate = remote(GU.at[0], GUX.at[0], x_send.at[3], x_recv.at[3], sibling)
    take(h_recv.at[2], GU.at[1, some_groups])

    def row_grad(rs):
        RG[rs, :] = (
            dot(GU[0, rs, :], weight(0), NT) + dot(GU[1, rs, :], weight(1), NT)
        ).astype(BF16)

    row_loop(row_grad)
    out_to_sources(RG, CB, 3)
    x_up = remote(GU.at[1], GUX.at[1], x_send.at[4], x_recv.at[4], sibling)
    x_gate.wait_recv()
    gg_out[...] = (
        dot(R[:, keep], GU[0], TN) + dot(RX[...], GUX[0], TN)
    ) * factor
    x_up.wait_recv()
    ug_out[...] = (
        dot(R[:, keep], GU[1], TN) + dot(RX[...], GUX[1], TN)
    ) * factor
    arrived(3)
    cb_out[...] = CB[...]

    for c in sent_w + [x_rows, x_hidden, x_grad, x_gate, x_up]:
        c.wait_send()
    for i in range(4):
        take(a_send.at[i], R.at[some])
    for i in range(2):
        take(p_send.at[i], PR.at[i])
    take(p_send.at[2], HR)
    for i in range(3):
        take(h_send.at[i], H.at[some_groups])


def on_device(
    tokens, target, route_index, route_count, route_gate, gate_weight, up_weight, down_weight
):
    groups = lax.axis_size("dp")
    experts = lax.axis_size("expert")
    planes = groups // CORES
    local_index = route_index[0, :, 0, :]
    live_count = route_count[0, :, 0]
    slots = local_index.shape[1]
    width = tokens.shape[1]
    half, _, ff = gate_weight.shape
    chunk = CORES * half
    usable = jnp.arange(slots, dtype=jnp.int32)[None, :] < live_count[:, None]
    slot_weight = jnp.where(usable, route_gate[0, :, 0, :], 0.0).reshape(-1)
    index = local_index.reshape(-1)
    rows = jnp.where(usable.reshape(-1)[:, None], tokens[index], jnp.zeros((), tokens.dtype))
    tgt = target[index]
    same = index[:, None] == index[None, :]
    amat = jnp.where(same, slot_weight[None, :], 0.0)
    picked = experts * slots
    all_rows = planes * picked
    vmem = pl.BlockSpec(memory_space=pltpu.VMEM)
    dma = pltpu.SemaphoreType.DMA
    came_back, gate_gradient, up_gradient, down_gradient = pl.pallas_call(
        functools.partial(
            kernel, planes, experts, slots, (groups * experts * slots) ** (-0.5)
        ),
        out_shape=(
            jax.ShapeDtypeStruct((picked, width), BF16),
            jax.ShapeDtypeStruct((half, ff), F32),
            jax.ShapeDtypeStruct((half, ff), F32),
            jax.ShapeDtypeStruct((half, ff), F32),
        ),
        in_specs=[vmem] * 7,
        out_specs=(vmem,) * 4,
        scratch_shapes=[
            pltpu.VMEM((3, CORES, half, ff), BF16),
            pltpu.VMEM((all_rows, chunk), BF16),
            pltpu.VMEM((all_rows, chunk), BF16),
            pltpu.VMEM((picked, width), BF16),
            pltpu.VMEM((picked, width), BF16),
            pltpu.VMEM((all_rows, chunk), BF16),
            pltpu.VMEM((all_rows, chunk), BF16),
            pltpu.VMEM((picked, width), BF16),
            pltpu.VMEM((2, all_rows, ff), BF16),
            pltpu.VMEM((2, planes - 1, picked, ff), BF16),
            pltpu.VMEM((all_rows, ff), BF16),
            pltpu.VMEM((planes - 1, picked, ff), BF16),
            pltpu.VMEM((all_rows, ff), BF16),
            pltpu.VMEM((2, all_rows, ff), BF16),
            pltpu.VMEM((all_rows, half), BF16),
            pltpu.VMEM((all_rows, half), BF16),
            pltpu.VMEM((all_rows, ff), BF16),
            pltpu.VMEM((2, all_rows, ff), BF16),
            dma((3,)), dma((3,)), dma((3,)),
            dma((4,)), dma((4,)), dma((4,)),
            dma((3,)), dma((3,)),
            dma((3,)), dma((3,)),
            dma((5,)), dma((5,)),
        ],
        compiler_params=pltpu.CompilerParams(
            collective_id=0, has_side_effects=True, vmem_limit_bytes=66000000
        ),
        name="routed_layer",
    )(
        rows, tgt, amat, slot_weight[:, None],
        gate_weight.reshape(half, ff), up_weight.reshape(half, ff),
        down_weight.reshape(half, ff),
    )
    spread = (
        jnp.arange(tokens.shape[0], dtype=jnp.int32)[:, None] == index[None, :]
    ).astype(BF16)
    token_grad = dot(spread, came_back, NN).astype(BF16)
    return (
        token_grad,
        gate_gradient.reshape(half, 1, ff),
        up_gradient.reshape(half, 1, ff),
        down_gradient.reshape(half, 1, ff),
    )


def solution(mesh):
    return jax.shard_map(
        on_device,
        mesh=mesh,
        in_specs=(
            P(("dp", "expert"), None),
            P(("dp", "expert"), None),
            P("dp", None, "expert", None),
            P("dp", None, "expert"),
            P("dp", None, "expert", None),
            P("dp", "expert", None),
            P("dp", "expert", None),
            P("dp", "expert", None),
        ),
        out_specs=(
            P(("dp", "expert"), None),
            P("dp", "expert", None),
            P("dp", "expert", None),
            P("dp", "expert", None),
        ),
        check_vma=False,
    )
```

time: 307 us -> 127 us (0.41)
  Pallas kernels: 0 us -> 100 us
  waiting for transfers between devices: 80.1 us -> 0 us
  other arithmetic: 62 us -> 5.54 us
  blocking collectives: 52.9 us -> 0 us
  local copies, waits for them, and re-layouts: 50.3 us -> 17.6 us
  starting transfers between devices: 26.7 us -> 0 us
  matrix products: 19.3 us -> 2.63 us
  between operations: 13.9 us -> 0.68 us
    pallas_call x0 -> x1, Pallas kernels: none -> 100 us  [on_device(): pl.pallas_call(functools.partial(kernel, planes, experts, slots, (groups...]
    all_gather x3 -> x0, waiting for transfers between devices: 59.7 us -> none  [the longest x1 35.6 us: on_device(): lax.all_gather(down_weight, 'dp', axis=0, tiled=True)]
    all_gather x3 -> x0, blocking collectives: 52.9 us -> none  [the longest x1 19.9 us: on_device(): up_piece = lax.all_gather(up_grad, 'dp', axis=1, tiled=True)]
    unnamed x6 -> x2, other arithmetic: 35.6 us -> 2.69 us
    all_to_all x6 -> x0, starting transfers between devices: 26.6 us -> none  [the longest x2 9.24 us: to_owners(): lax.all_to_all(block, 'expert', split_axis=0, concat_axis=1, tiled=True)]
    unnamed x32 -> x9, local copies, waits for them, and re-layouts: 31.1 us -> 8.45 us
    all_to_all x6 -> x0, waiting for transfers between devices: 18.3 us -> none  [the longest x1 8.38 us: on_device(): lax.all_to_all(expert_rows, 'dp', split_axis=2, concat_axis=1, tiled=True)]
    dot_general x9 -> x1, matrix products: 19.3 us -> 2.63 us  [dot(): lax.dot_general(a, b, (dims, ((), ())), preferred_element_type=F32, preci...]
  transfers between devices with their start and end apart: 9 -> 0, of which waited for: 5 -> 0; matrix products, arithmetic and copies ran while one was open for 25% -> 0% of each run, Pallas kernels for 0% -> 0%
where the time goes in v1:
time: 127 us
  Pallas kernels  100 us (79%)
  local copies, waits for them, and re-layouts  17.6 us (14%)
  other arithmetic  5.54 us (4%)
  matrix products  2.63 us (2%)
    pallas_call x1, Pallas kernels, on_device(): pl.pallas_call(functools.partial(kernel, planes, experts, slots, (groups...  100 us
    unnamed x9, local copies, waits for them, and re-layouts  8.45 us
    gather x1, local copies, waits for them, and re-layouts, on_device(): tgt = target[index]  3.98 us
    gather x1, local copies, waits for them, and re-layouts, on_device(): tokens[index]  3.28 us
    unnamed x2, other arithmetic  2.69 us
    dot_general x1, matrix products, dot(): lax.dot_general(a, b, (dims, ((), ())), preferred_element_type=F32, preci...  2.63 us

profile of v1, /device:TPU:0, one launch (start us, length us, event | category | flops | bytes accessed | tf_op | source)
XLA Modules:
  0.0 126.5 jit_solution(947380058167238241)
XLA Ops:
  0.6 0.7 iota_compare_fusion.2
  1.4 0.1 lt.50
  1.4 0.8 reshape_squeeze.3
  2.2 0.5 broadcast.64
  2.7 1.3 %reduce.11 = s32[4,16]{1,0:T(4,128)S(1)} reduce(s32[1,4,1,16]{3,2,1,0:T(1,128)} %param.10, s32[]{:T(128)} %broadcast.64), dimensions={0,2}, to_apply=%param.10.reduce_sub_computation.5 | reduce | bytes 516 | tf_op args[2]
  4.1 0.1 eq.29
  4.2 0.5 broadcast.63
  4.7 1.3 %reduce.10 = f32[4,16]{1,0:T(4,128)S(1)} reduce(f32[1,4,1,16]{3,2,1,0:T(1,128)} %param.12, f32[]{:T(128)} %broadcast.63), dimensions={0,2}, to_apply=%param.12.reduce_sub_computation.5 | reduce | bytes 516 | tf_op args[4]
  6.0 0.1 squeeze.5
  6.1 0.1 lt.53
  6.2 0.7 compare_select_fusion.amat
  6.9 0.8 squeeze.7
  7.7 0.6 broadcast_select_fusion.1.wcol
  8.3 4.0 %gather_fusion.1 = bf16[64,2048]{1,0:T(8,128)(2,1)} fusion(bf16[768,2048]{1,0:T(8,128)(2,1)} %param.9, s32[1024]{0:T(1024)S(1)} %pad_clamp_fusion), kind=kCustom, calls=%fused_computation.1 | custom fusion | bytes 524544 | tf_op jit(solution)/shard_map/gather | solution.py:284
  12.3 3.3 %gather_fusion = bf16[64,2048]{1,0:T(8,128)(2,1)S(1)} fusion(bf16[768,2048]{1,0:T(8,128)(2,1)} %param.8, s32[1024]{0:T(1024)S(1)} %pad_clamp_fusion), kind=kCustom, calls=%fused_computation | custom fusion | bytes 524544 | tf_op jit(solution)/shard_map/gather | solution.py:283
  15.6 0.8 broadcast_select_fusion.rows
  16.4 100.1 %routed_layer.1 = (bf16[64,2048]{1,0:T(8,128)(2,1)}, f32[256,768]{1,0:T(8,128)}, f32[256,768]{1,0:T(8,128)}, f32[256,768]{1,0:T(8,128)}) custom-call(bf16[64,2048]{1,0:T(8,128)(2,1)} %broadcast_select_fusion.rows, bf16[64,2048]{1,0:T(8,128)(2,1)} %gather_fusion.1, f32[64,64]{1,0:T(8,128)} %compare_select_fusion.amat, f32[64,1]{1,0:T(8,128)} %broadcast_select_fusion.1.wcol, ...), custom_call_target="tpu_custom_call" | custom-call | tf_op jit(solution)/shard_map/routed_layer/pallas_call | solution.py:291
  116.5 0.0 copy-start
  116.5 0.0 copy-start.1
  116.5 2.9 %copy.14 = f32[256,1,768]{2,1,0:T(1,128)} copy(f32[256,1,768]{2,0,1:T(8,128)} %bitcast.14) | data formatting | bytes 1572864
  119.4 2.8 %copy.15 = f32[256,1,768]{2,1,0:T(1,128)} copy(f32[256,1,768]{2,0,1:T(8,128)} %bitcast.13) | data formatting | bytes 1572864
  122.2 0.0 copy-done
  122.2 1.7 %copy.16 = f32[256,1,768]{2,1,0:T(1,128)} copy(f32[256,1,768]{2,0,1:T(8,128)S(1)} %bitcast.12) | data formatting | bytes 1572864
  123.9 0.0 copy-done.1
  123.9 2.6 %convolution_convert_fusion = bf16[768,2048]{1,0:T(8,128)(2,1)} fusion(bf16[64,2048]{1,0:T(8,128)(2,1)S(1)} %copy-done.1, s32[64]{0:T(128)S(1)} %eq.29), kind=kOutput, calls=%fused_computation.2 | convolution fusion | flops 202948608 | bytes 3408128 | tf_op jit(solution)/shard_map/dot_general | solution.py:16
  (3 shorter events, 0.0 us)
Async XLA Ops:
  116.5 5.8 %copy-start = (f32[256,768]{1,0:T(8,128)S(1)}, f32[256,768]{1,0:T(8,128)}, u32[]{:S(2)}) copy-start(f32[256,768]{1,0:T(8,128)} %get-tuple-element.11) | copy-start | bytes 2359300
  116.5 7.4 %copy-start.1 = (bf16[64,2048]{1,0:T(8,128)(2,1)S(1)}, bf16[64,2048]{1,0:T(8,128)(2,1)}, u32[]{:S(2)}) copy-start(bf16[64,2048]{1,0:T(8,128)(2,1)} %get-tuple-element.8) | copy-start | bytes 786436

commit v2 on v1

v2 whole, which is shorter than its diff:
```python
import functools

import jax
import jax.numpy as jnp
from jax import lax
from jax.experimental import pallas as pl
from jax.experimental.pallas import tpu as pltpu
from jax.sharding import PartitionSpec as P

F32 = jnp.float32
BF16 = jnp.bfloat16
VMEM_LIMIT = 67000000
CORES = 2


def dot(a, b, dims, precision=None):
    return lax.dot_general(
        a, b, (dims, ((), ())), preferred_element_type=F32, precision=precision
    )


NN = ((1,), (0,))
NT = ((1,), (1,))
TN = ((0,), (0,))


def kernel(
    planes, experts, slots, factor,
    index, count, gate, tokens, target, gw, uw, dw,
    cb_out, hot_out, gg_out, ug_out, dg_out,
    TOK, TGT, ROWS, TROWS, W, R, EO, RET, SG, G, RG, CB, PS, PR, H, GU, RX, GX, HX, GUX,
    t_loc, g_loc, w_loc, w_send, w_recv, a_loc, a_send, a_recv, p_send, p_recv,
    h_send, h_recv, x_send, x_recv,
):
    dp = lax.axis_index("dp")
    me_e = lax.axis_index("expert")
    me_z = dp // CORES
    core = dp % CORES
    peers = planes * experts
    per_group = experts * slots
    half = gw.shape[0]
    chunk = CORES * half
    ff = gw.shape[1]
    me = me_z * experts + me_e
    sibling = {"dp": me_z * CORES + (1 - core), "expert": me_e}
    order = sorted(range(1, planes), key=lambda k: -min(k, planes - k))

    def at(z, e):
        return {"dp": z * CORES + core, "expert": e}

    def plane(k):
        return (me_z + k) % planes

    def slot_rows(n):
        return pl.ds(pl.multiple_of(n * slots, slots), slots)

    def cols(z):
        return pl.ds(pl.multiple_of(z * chunk, chunk), chunk)

    def group_rows(z):
        return pl.ds(pl.multiple_of(z * per_group, per_group), per_group)

    barrier = pltpu.get_barrier_semaphore()

    def greet(k, carry):
        p = (me + k) % peers
        pl.semaphore_signal(
            barrier, inc=1, device_id=at(p // experts, p % experts),
            device_id_type=pl.DeviceIdType.MESH,
        )
        return carry

    lax.fori_loop(1, peers, greet, 0)
    pl.semaphore_signal(
        barrier, inc=1, device_id=sibling, device_id_type=pl.DeviceIdType.MESH
    )
    tok_copies = {}
    for k in order + [0]:
        z = plane(k)
        tok_copies[k] = pltpu.make_async_copy(
            tokens.at[:, cols(z)], TOK.at[:, cols(z)], t_loc.at[k]
        )
        tok_copies[k].start()
    locals_w = []
    for i, w in enumerate((gw, uw, dw)):
        c = pltpu.make_async_copy(w, W.at[i, core], w_loc.at[i])
        c.start()
        locals_w.append(c)
    tgt_copy = pltpu.make_async_copy(target, TGT, g_loc)
    tgt_copy.start()

    lane = lax.broadcasted_iota(jnp.int32, (slots, slots), 1)
    own_lane = lane == lax.broadcasted_iota(jnp.int32, (slots, slots), 0)
    slot_id = lax.broadcasted_iota(jnp.int32, (slots, 1), 0)
    names, weights = [], []
    for e in range(experts):
        live = slot_id < jnp.broadcast_to(count[0:1, e : e + 1], (slots, 1))
        ids = jnp.broadcast_to(index[0, e], (slots, slots))
        ids = jnp.sum(jnp.where(own_lane, ids, 0), axis=1, keepdims=True)
        names.append(jnp.where(live, ids, -1))
        g = jnp.broadcast_to(gate[0, e], (slots, slots))
        g = jnp.sum(jnp.where(own_lane, g, 0.0), axis=1, keepdims=True)
        weights.append(jnp.where(live, g, 0.0))
    names = jnp.concatenate(names, axis=0)
    wcol = jnp.concatenate(weights, axis=0)
    hot = (
        names == lax.broadcasted_iota(jnp.int32, (per_group, TOK.shape[0]), 1)
    ).astype(F32).astype(BF16)
    hot_out[...] = hot

    def remote(src, dst, s, r, dev):
        c = pltpu.make_async_remote_copy(
            src_ref=src, dst_ref=dst, send_sem=s, recv_sem=r,
            device_id=dev, device_id_type=pl.DeviceIdType.MESH,
        )
        c.start()
        return c

    def to_plane(i, k, source, land):
        z = plane(k)
        first = 0
        if k == 0:
            pltpu.make_async_copy(source(z, me_e), land, a_loc.at[i]).start()
            first = 1

        def send(j, carry):
            e = (me_e + j) % experts
            remote(source(z, e), land, a_send.at[i], a_recv.at[i, me_z], at(z, e))
            return carry

        lax.fori_loop(first, experts, send, 0)

    def owners(src, dst, i, k):
        to_plane(i, k, lambda z, e: src.at[slot_rows(e), cols(z)], dst.at[slot_rows(me)])

    def sources(src, dst, i, k):
        to_plane(
            i, k, lambda z, e: src.at[slot_rows(z * experts + e)],
            dst.at[slot_rows(me_e), cols(me_z)],
        )

    def take(sem, ref):
        pltpu.make_async_copy(ref, ref, sem).wait()

    def arrived(i, k):
        if k == 0:
            take(a_recv.at[i, me_z], R.at[pl.ds(0, (experts - 1) * slots)])
            take(a_loc.at[i], R.at[pl.ds(0, slots)])
        else:
            take(a_recv.at[i, plane(k)], R.at[pl.ds(0, per_group)])

    def weight(i):
        return W[i].reshape(chunk, ff)

    pl.semaphore_wait(barrier, peers)
    for k in order + [0]:
        z = plane(k)
        tok_copies[k].wait()
        ROWS[:, cols(z)] = dot(hot, TOK[:, cols(z)], NN).astype(BF16)
        owners(ROWS, R, 0, k)
    sent_w = [
        remote(w, W.at[i, core], w_send.at[i], w_recv.at[i], sibling)
        for i, w in enumerate((gw, uw, dw))
    ]

    def send_sum(i, k):
        remote(
            PS.at[i, group_rows(plane(k))], PR.at[i, k - 1],
            p_send.at[i], p_recv.at[i, k - 1], at(plane(k), me_e),
        )

    def spread(buf, i):
        mine = buf.at[group_rows(me_z)]
        for k in order:
            remote(mine, mine, h_send.at[i], h_recv.at[i, me_z], at(plane(k), me_e))

    def total(i, own):
        for k in order:
            take(p_recv.at[i, k - 1], PR.at[i, k - 1])
            own = own + PR[i, k - 1].astype(F32)
        return own

    keep = pl.ds(pl.multiple_of(core * half, half), half)
    give = pl.ds(pl.multiple_of((1 - core) * half, half), half)
    mine = group_rows(me_z)

    for i in range(2):
        locals_w[i].wait()
        sent_w[i].wait_recv()
    for k in order:
        z = plane(k)
        arrived(0, k)
        for i in range(2):
            PS[i, group_rows(z), :] = dot(R[group_rows(z), :], weight(i), NN).astype(BF16)
            send_sum(i, k)
    arrived(0, 0)
    gate_own = dot(R[mine, :], weight(0), NN)
    up_own = dot(R[mine, :], weight(1), NN)
    x_rows = remote(R.at[:, give], RX, x_send.at[0], x_recv.at[0], sibling)
    tgt_copy.wait()
    for z in range(planes):
        piece = slice(z * chunk, (z + 1) * chunk)
        TROWS[:, piece] = dot(hot, TGT[:, piece], NN)
    same = dot(hot, hot, NT).astype(BF16)
    gate_pre = total(0, gate_own)
    up_pre = total(1, up_own)
    sigma = jax.nn.sigmoid(gate_pre)
    active = gate_pre * sigma
    H[mine, :] = (active * up_pre).astype(BF16)
    spread(H, 0)
    locals_w[2].wait()
    sent_w[2].wait_recv()
    some_groups = pl.ds(0, (planes - 1) * per_group)

    for k in [0] + order:
        z = plane(k)
        if k:
            take(h_recv.at[0, z], H.at[group_rows(z)])
        EO[group_rows(z), :] = dot(H[group_rows(z), :], weight(2), NT).astype(BF16)
        sources(EO, RET, 1, k)
    x_hidden = remote(H, HX, x_send.at[1], x_recv.at[1], sibling)
    for k in order + [0]:
        z = plane(k)
        arrived(1, k)
        part = wcol * RET[:, cols(z)].astype(F32)
        combined = -TROWS[:, cols(z)]
        for _ in range(3):
            top = part.astype(BF16)
            combined = combined + dot(same, top, NN)
            part = part - top.astype(F32)
        SG[:, cols(z)] = (wcol * combined).astype(BF16)
        owners(SG, G, 2, k)

    for k in order:
        z = plane(k)
        arrived(2, k)
        PS[2, group_rows(z), :] = dot(G[group_rows(z), :], weight(2), NN).astype(BF16)
        send_sum(2, k)
    arrived(2, 0)
    own = dot(G[mine, :], weight(2), NN)
    x_grad = remote(G.at[:, give], GX, x_send.at[2], x_recv.at[2], sibling)
    x_hidden.wait_recv()
    x_grad.wait_recv()
    dg_out[...] = (dot(G[:, keep], H[...], TN) + dot(GX[...], HX[...], TN)) * factor
    hidden_grad = total(2, own)
    GU[0, mine, :] = (
        hidden_grad * up_pre * sigma * (1.0 + gate_pre * (1.0 - sigma))
    ).astype(BF16)
    spread(GU.at[0], 1)
    GU[1, mine, :] = (hidden_grad * active).astype(BF16)
    spread(GU.at[1], 2)

    for k in [0] + order:
        z = plane(k)
        if k:
            take(h_recv.at[1, z], H.at[group_rows(z)])
            take(h_recv.at[2, z], H.at[group_rows(z)])
        RG[group_rows(z), :] = (
            dot(GU[0, group_rows(z), :], weight(0), NT)
            + dot(GU[1, group_rows(z), :], weight(1), NT)
        ).astype(BF16)
        sources(RG, CB, 3, k)
    x_gate = remote(GU.at[0], GUX.at[0], x_send.at[3], x_recv.at[3], sibling)
    x_up = remote(GU.at[1], GUX.at[1], x_send.at[4], x_recv.at[4], sibling)
    x_rows.wait_recv()
    x_gate.wait_recv()
    gg_out[...] = (
        dot(R[:, keep], GU[0], TN) + dot(RX[...], GUX[0], TN)
    ) * factor
    x_up.wait_recv()
    ug_out[...] = (
        dot(R[:, keep], GU[1], TN) + dot(RX[...], GUX[1], TN)
    ) * factor
    for k in order + [0]:
        arrived(3, k)
    cb_out[...] = CB[...]

    for c in sent_w + [x_rows, x_hidden, x_grad, x_gate, x_up]:
        c.wait_send()
    for i in range(4):
        take(a_send.at[i], R.at[pl.ds(0, (peers - 1) * slots)])
    for i in range(3):
        take(p_send.at[i], PR.at[i])
        take(h_send.at[i], H.at[some_groups])


def finish(hot, cb, gg, ug, dg, tg_out, gg_out, ug_out, dg_out):
    tg_out[...] = dot(hot[...], cb[...], TN).astype(BF16)
    gg_out[:, 0, :] = gg[...]
    ug_out[:, 0, :] = ug[...]
    dg_out[:, 0, :] = dg[...]


def on_device(
    tokens, target, route_index, route_count, route_gate, gate_weight, up_weight, down_weight
):
    groups = lax.axis_size("dp")
    experts = lax.axis_size("expert")
    planes = groups // CORES
    slots = route_index.shape[3]
    count, width = tokens.shape
    half, _, ff = gate_weight.shape
    chunk = CORES * half
    picked = experts * slots
    all_rows = planes * picked
    vmem = pl.BlockSpec(memory_space=pltpu.VMEM)
    anyw = pl.BlockSpec(memory_space=pl.ANY)
    dma = pltpu.SemaphoreType.DMA
    grad = jax.ShapeDtypeStruct((half, ff), F32)
    came_back, hot, gate_gradient, up_gradient, down_gradient = pl.pallas_call(
        functools.partial(
            kernel, planes, experts, slots, (groups * experts * slots) ** (-0.5)
        ),
        out_shape=(
            jax.ShapeDtypeStruct((picked, width), BF16),
            jax.ShapeDtypeStruct((picked, count), BF16),
            grad, grad, grad,
        ),
        in_specs=[vmem] * 3 + [anyw] * 5,
        out_specs=(vmem,) * 5,
        scratch_shapes=[
            pltpu.VMEM((count, width), BF16),
            pltpu.VMEM((count, width), BF16),
            pltpu.VMEM((picked, width), BF16),
            pltpu.VMEM((picked, width), F32),
            pltpu.VMEM((3, CORES, half, ff), BF16),
            pltpu.VMEM((all_rows, chunk), BF16),
            pltpu.VMEM((all_rows, chunk), BF16),
            pltpu.VMEM((picked, width), BF16),
            pltpu.VMEM((picked, width), BF16),
            pltpu.VMEM((all_rows, chunk), BF16),
            pltpu.VMEM((all_rows, chunk), BF16),
            pltpu.VMEM((picked, width), BF16),
            pltpu.VMEM((3, all_rows, ff), BF16),
            pltpu.VMEM((3, planes - 1, picked, ff), BF16),
            pltpu.VMEM((all_rows, ff), BF16),
            pltpu.VMEM((2, all_rows, ff), BF16),
            pltpu.VMEM((all_rows, half), BF16),
            pltpu.VMEM((all_rows, half), BF16),
            pltpu.VMEM((all_rows, ff), BF16),
            pltpu.VMEM((2, all_rows, ff), BF16),
            dma((planes,)), dma,
            dma((3,)), dma((3,)), dma((3,)),
            dma((4,)), dma((4,)), dma((4, planes)),
            dma((3,)), dma((3, planes)),
            dma((3,)), dma((3, planes)),
            dma((5,)), dma((5,)),
        ],
        compiler_params=pltpu.CompilerParams(
            collective_id=0, has_side_effects=True, vmem_limit_bytes=VMEM_LIMIT
        ),
        name="routed_layer",
    )(
        route_index, route_count.reshape(1, experts), route_gate, tokens, target,
        gate_weight.reshape(half, ff), up_weight.reshape(half, ff),
        down_weight.reshape(half, ff),
    )
    steps = 2
    part = pl.BlockSpec((half // steps, ff), lambda i: (i, 0))
    part_out = pl.BlockSpec((half // steps, 1, ff), lambda i: (i, 0, 0))
    grad = jax.ShapeDtypeStruct((half, 1, ff), F32)
    return tuple(pl.pallas_call(
        finish,
        grid=(steps,),
        out_shape=(jax.ShapeDtypeStruct((count, width), BF16), grad, grad, grad),
        in_specs=[
            pl.BlockSpec((picked, count // steps), lambda i: (0, i)),
            pl.BlockSpec((picked, width), lambda i: (0, 0)),
            part, part, part,
        ],
        out_specs=(
            pl.BlockSpec((count // steps, width), lambda i: (i, 0)),
            part_out, part_out, part_out,
        ),
        compiler_params=pltpu.CompilerParams(vmem_limit_bytes=32000000),
        name="finish",
    )(hot, came_back, gate_gradient, up_gradient, down_gradient))


def solution(mesh):
    return jax.shard_map(
        on_device,
        mesh=mesh,
        in_specs=(
            P(("dp", "expert"), None),
            P(("dp", "expert"), None),
            P("dp", None, "expert", None),
            P("dp", None, "expert"),
            P("dp", None, "expert", None),
            P("dp", "expert", None),
            P("dp", "expert", None),
            P("dp", "expert", None),
        ),
        out_specs=(
            P(("dp", "expert"), None),
            P("dp", "expert", None),
            P("dp", "expert", None),
            P("dp", "expert", None),
        ),
        check_vma=False,
    )
```

time: 127 us -> 97.1 us (0.76)
  local copies, waits for them, and re-layouts: 17.6 us -> 5.23 us
  Pallas kernels: 100 us -> 90.9 us
  other arithmetic: 5.54 us -> 0 us
  matrix products: 2.63 us -> 0 us
    pallas_call x1, Pallas kernels: 100 us -> 87.9 us  [on_device(): pl.pallas_call(functools.partial(kernel, planes, experts, slots, (groups...]
    gather x2 -> x0, local copies, waits for them, and re-layouts: 7.26 us -> none  [the longest x1 3.98 us: on_device(): tgt = target[index]]
    unnamed x9 -> x10, local copies, waits for them, and re-layouts: 8.45 us -> 5.23 us
    pallas_call x0 -> x1, Pallas kernels: none -> 3.04 us  [on_device(): pl.pallas_call(finish, grid=(steps,), out_shape=(jax.ShapeDtypeStruct((co...]
    unnamed x2 -> x0, other arithmetic: 2.69 us -> none
    dot_general x1 -> x0, matrix products: 2.63 us -> none  [dot(): lax.dot_general(a, b, (dims, ((), ())), preferred_element_type=F32, preci...]
    select_n x5 -> x0, other arithmetic: 2.12 us -> none  [the longest x1 0.79 us: on_device(): jnp.where(usable.reshape(-1)[:, None], tokens[index], jnp.zeros((), token...]
where the time goes in v2:
time: 97.1 us; the launch traced here: 96.8 us
  Pallas kernels  90.9 us (94%)
  local copies, waits for them, and re-layouts  5.23 us (5%)
    pallas_call x1, Pallas kernels, on_device(): pl.pallas_call(functools.partial(kernel, planes, experts, slots, (groups...  87.9 us
    unnamed x10, local copies, waits for them, and re-layouts  5.23 us
    pallas_call x1, Pallas kernels, on_device(): pl.pallas_call(finish, grid=(steps,), out_shape=(jax.ShapeDtypeStruct((co...  3.04 us

profile of v2, /device:TPU:0, one launch (start us, length us, event | category | flops | bytes accessed | tf_op | source)
XLA Modules:
  0.0 96.8 jit_solution(14744495518411946828)
XLA Ops:
  0.6 87.9 %routed_layer.1 = (bf16[64,2048]{1,0:T(8,128)(2,1)}, bf16[64,768]{1,0:T(8,128)(2,1)}, f32[256,768]{1,0:T(8,128)}, f32[256,768]{1,0:T(8,128)}, f32[256,768]{1,0:T(8,128)}) custom-call(s32[1,4,1,16]{3,2,1,0:T(1,128)} %index.1, s32[1,4]{1,0:T(1,128)} %bitcast.7, f32[1,4,1,16]{3,2,1,0:T(1,128)} %gate.1, bf16[768,2048]{1,0:T(8,128)(2,1)} %tokens.1, ...), custom_call_target="tpu_custom_call" | custom-call | tf_op jit(solution)/shard_map/routed_layer/pallas_call | solution.py:310
  88.5 0.0 copy-start
  88.5 1.1 %copy-done = f32[256,768]{1,0:T(8,128)S(1)} copy-done((f32[256,768]{1,0:T(8,128)S(1)}, f32[256,768]{1,0:T(8,128)}, u32[]{:S(2)}) %copy-start) | copy-done | bytes 786456
  89.6 0.0 copy-start.1
  89.6 1.1 %copy-done.1 = f32[256,768]{1,0:T(8,128)S(1)} copy-done((f32[256,768]{1,0:T(8,128)S(1)}, f32[256,768]{1,0:T(8,128)}, u32[]{:S(2)}) %copy-start.1) | copy-done | bytes 786456
  90.8 0.0 copy-start.2
  90.8 1.1 %copy-done.2 = f32[256,768]{1,0:T(8,128)S(1)} copy-done((f32[256,768]{1,0:T(8,128)S(1)}, f32[256,768]{1,0:T(8,128)}, u32[]{:S(2)}) %copy-start.2) | copy-done | bytes 786456
  91.9 0.0 copy-start.3
  91.9 0.9 copy-done.3
  92.9 0.0 copy-start.4
  92.9 0.9 copy-done.4
  93.8 3.0 %finish.1 = (bf16[768,2048]{1,0:T(8,128)(2,1)}, f32[256,1,768]{2,1,0:T(1,128)}, f32[256,1,768]{2,1,0:T(1,128)}, f32[256,1,768]{2,1,0:T(1,128)}) custom-call(bf16[64,768]{1,0:T(8,128)(2,1)S(1)} %copy-done.4, bf16[64,2048]{1,0:T(8,128)(2,1)S(1)} %copy-done.3, f32[256,768]{1,0:T(8,128)S(1)} %copy-done, f32[256,768]{1,0:T(8,128)S(1)} %copy-done.1, ...), custom_call_target="tpu_custom_call" | custom-call | tf_op jit(solution)/shard_map/finish/pallas_call | solution.py:362
Async XLA Ops:
  88.5 1.1 %copy-start = (f32[256,768]{1,0:T(8,128)S(1)}, f32[256,768]{1,0:T(8,128)}, u32[]{:S(2)}) copy-start(f32[256,768]{1,0:T(8,128)} %get-tuple-element.11.gg) | copy-start | bytes 2359300
  89.6 1.1 %copy-start.1 = (f32[256,768]{1,0:T(8,128)S(1)}, f32[256,768]{1,0:T(8,128)}, u32[]{:S(2)}) copy-start(f32[256,768]{1,0:T(8,128)} %get-tuple-element.12.ug) | copy-start | bytes 2359300
  90.8 1.1 %copy-start.2 = (f32[256,768]{1,0:T(8,128)S(1)}, f32[256,768]{1,0:T(8,128)}, u32[]{:S(2)}) copy-start(f32[256,768]{1,0:T(8,128)} %get-tuple-element.13.dg) | copy-start | bytes 2359300
  91.9 0.9 copy-start.3
  92.9 0.9 copy-start.4

commit v3 on v2

--- a/solution.py
+++ b/solution.py
@@ -30,7 +30,7 @@
     cb_out, hot_out, gg_out, ug_out, dg_out,
     TOK, TGT, ROWS, TROWS, W, R, EO, RET, SG, G, RG, CB, PS, PR, H, GU, RX, GX, HX, GUX,
     t_loc, g_loc, w_loc, w_send, w_recv, a_loc, a_send, a_recv, p_send, p_recv,
-    h_send, h_recv, x_send, x_recv,
+    h_send, h_recv, x_send, x_recv, GRADS, o_loc,
 ):
     dp = lax.axis_index("dp")
     me_e = lax.axis_index("expert")
@@ -116,12 +116,14 @@
         c.start()
         return c
 
-    def to_plane(i, k, source, land):
-        z = plane(k)
-        first = 0
-        if k == 0:
-            pltpu.make_async_copy(source(z, me_e), land, a_loc.at[i]).start()
-            first = 1
+    def to_plane(i, z, source, land):
+        here = z == me_z
+
+        @pl.when(here)
+        def _():
+            pltpu.make_async_copy(source(me_z, me_e), land, a_loc.at[i]).start()
+
+        first = jnp.where(here, 1, 0)
 
         def send(j, carry):
             e = (me_e + j) % experts
@@ -130,12 +132,12 @@
 
         lax.fori_loop(first, experts, send, 0)
 
-    def owners(src, dst, i, k):
-        to_plane(i, k, lambda z, e: src.at[slot_rows(e), cols(z)], dst.at[slot_rows(me)])
-
-    def sources(src, dst, i, k):
+    def owners(src, dst, i, z):
+        to_plane(i, z, lambda z, e: src.at[slot_rows(e), cols(z)], dst.at[slot_rows(me)])
+
+    def sources(src, dst, i, z):
         to_plane(
-            i, k, lambda z, e: src.at[slot_rows(z * experts + e)],
+            i, z, lambda z, e: src.at[slot_rows(z * experts + e)],
             dst.at[slot_rows(me_e), cols(me_z)],
         )
 
@@ -149,6 +151,13 @@
         else:
             take(a_recv.at[i, plane(k)], R.at[pl.ds(0, per_group)])
 
+    outs = []
+
+    def put(i, src, dst):
+        c = pltpu.make_async_copy(src, dst, o_loc.at[i])
+        c.start()
+        outs.append(c)
+
     def weight(i):
         return W[i].reshape(chunk, ff)
 
@@ -157,7 +166,7 @@
         z = plane(k)
         tok_copies[k].wait()
         ROWS[:, cols(z)] = dot(hot, TOK[:, cols(z)], NN).astype(BF16)
-        owners(ROWS, R, 0, k)
+        owners(ROWS, R, 0, z)
     sent_w = [
         remote(w, W.at[i, core], w_send.at[i], w_recv.at[i], sibling)
         for i, w in enumerate((gw, uw, dw))
@@ -169,10 +178,45 @@
             p_send.at[i], p_recv.at[i, k - 1], at(plane(k), me_e),
         )
 
+    def pass_on(buf, i, s, way):
+        to = me_z + way
+
+        @pl.when(jnp.logical_and(to >= 0, to < planes))
+        def _():
+            rows_s = buf.at[group_rows(s)]
+            remote(
+                rows_s, rows_s, h_send.at[i, (way + 1) // 2, s], h_recv.at[i, s],
+                at(to, me_e),
+            )
+
     def spread(buf, i):
-        mine = buf.at[group_rows(me_z)]
-        for k in order:
-            remote(mine, mine, h_send.at[i], h_recv.at[i, me_z], at(plane(k), me_e))
+        for way in (1, -1):
+            pass_on(buf, i, me_z, way)
+
+    def along(bufs, first, fn):
+        fn(me_z)
+        for far in range(1, planes):
+            for way in (1, -1):
+                s = me_z - way * far
+
+                @pl.when(jnp.logical_and(s >= 0, s < planes))
+                def _():
+                    for j, buf in enumerate(bufs):
+                        take(h_recv.at[first + j, s], buf.at[group_rows(s)])
+                        pass_on(buf, first + j, s, way)
+                    fn(s)
+
+    def spread_sent(buf, i):
+        for s in range(planes):
+            rows_s = buf.at[pl.ds(s * per_group, per_group)]
+
+            @pl.when(jnp.logical_and(me_z > 0, me_z <= s))
+            def _():
+                take(h_send.at[i, 0, s], rows_s)
+
+            @pl.when(jnp.logical_and(me_z < planes - 1, me_z >= s))
+            def _():
+                take(h_send.at[i, 1, s], rows_s)
 
     def total(i, own):
         for k in order:
@@ -210,14 +254,12 @@
     spread(H, 0)
     locals_w[2].wait()
     sent_w[2].wait_recv()
-    some_groups = pl.ds(0, (planes - 1) * per_group)
-
-    for k in [0] + order:
-        z = plane(k)
-        if k:
-            take(h_recv.at[0, z], H.at[group_rows(z)])
+
+    def expert_out(z):
         EO[group_rows(z), :] = dot(H[group_rows(z), :], weight(2), NT).astype(BF16)
-        sources(EO, RET, 1, k)
+        sources(EO, RET, 1, z)
+
+    along([H], 0, expert_out)
     x_hidden = remote(H, HX, x_send.at[1], x_recv.at[1], sibling)
     for k in order + [0]:
         z = plane(k)
@@ -229,7 +271,7 @@
             combined = combined + dot(same, top, NN)
             part = part - top.astype(F32)
         SG[:, cols(z)] = (wcol * combined).astype(BF16)
-        owners(SG, G, 2, k)
+        owners(SG, G, 2, z)
 
     for k in order:
         z = plane(k)
@@ -241,7 +283,8 @@
     x_grad = remote(G.at[:, give], GX, x_send.at[2], x_recv.at[2], sibling)
     x_hidden.wait_recv()
     x_grad.wait_recv()
-    dg_out[...] = (dot(G[:, keep], H[...], TN) + dot(GX[...], HX[...], TN)) * factor
+    GRADS[2] = (dot(G[:, keep], H[...], TN) + dot(GX[...], HX[...], TN)) * factor
+    put(2, GRADS.at[2], dg_out)
     hidden_grad = total(2, own)
     GU[0, mine, :] = (
         hidden_grad * up_pre * sigma * (1.0 + gate_pre * (1.0 - sigma))
@@ -250,30 +293,26 @@
     GU[1, mine, :] = (hidden_grad * active).astype(BF16)
     spread(GU.at[1], 2)
 
-    for k in [0] + order:
-        z = plane(k)
-        if k:
-            take(h_recv.at[1, z], H.at[group_rows(z)])
-            take(h_recv.at[2, z], H.at[group_rows(z)])
+    def row_grad(z):
         RG[group_rows(z), :] = (
             dot(GU[0, group_rows(z), :], weight(0), NT)
             + dot(GU[1, group_rows(z), :], weight(1), NT)
         ).astype(BF16)
-        sources(RG, CB, 3, k)
+        sources(RG, CB, 3, z)
+
+    along([GU.at[0], GU.at[1]], 1, row_grad)
     x_gate = remote(GU.at[0], GUX.at[0], x_send.at[3], x_recv.at[3], sibling)
     x_up = remote(GU.at[1], GUX.at[1], x_send.at[4], x_recv.at[4], sibling)
     x_rows.wait_recv()
     x_gate.wait_recv()
-    gg_out[...] = (
-        dot(R[:, keep], GU[0], TN) + dot(RX[...], GUX[0], TN)
-    ) * factor
+    GRADS[0] = (dot(R[:, keep], GU[0], TN) + dot(RX[...], GUX[0], TN)) * factor
+    put(0, GRADS.at[0], gg_out)
     x_up.wait_recv()
-    ug_out[...] = (
-        dot(R[:, keep], GU[1], TN) + dot(RX[...], GUX[1], TN)
-    ) * factor
+    GRADS[1] = (dot(R[:, keep], GU[1], TN) + dot(RX[...], GUX[1], TN)) * factor
+    put(1, GRADS.at[1], ug_out)
     for k in order + [0]:
         arrived(3, k)
-    cb_out[...] = CB[...]
+    put(3, CB, cb_out)
 
     for c in sent_w + [x_rows, x_hidden, x_grad, x_gate, x_up]:
         c.wait_send()
@@ -281,7 +320,10 @@
         take(a_send.at[i], R.at[pl.ds(0, (peers - 1) * slots)])
     for i in range(3):
         take(p_send.at[i], PR.at[i])
-        take(h_send.at[i], H.at[some_groups])
+    for i, buf in enumerate((H, GU.at[0], GU.at[1])):
+        spread_sent(buf, i)
+    for c in outs:
+        c.wait()
 
 
 def finish(hot, cb, gg, ug, dg, tg_out, gg_out, ug_out, dg_out):
@@ -317,7 +359,7 @@
             grad, grad, grad,
         ),
         in_specs=[vmem] * 3 + [anyw] * 5,
-        out_specs=(vmem,) * 5,
+        out_specs=(anyw, vmem) + (anyw,) * 3,
         scratch_shapes=[
             pltpu.VMEM((count, width), BF16),
             pltpu.VMEM((count, width), BF16),
@@ -343,8 +385,9 @@
             dma((3,)), dma((3,)), dma((3,)),
             dma((4,)), dma((4,)), dma((4, planes)),
             dma((3,)), dma((3, planes)),
-            dma((3,)), dma((3, planes)),
+            dma((3, 2, planes)), dma((3, planes)),
             dma((5,)), dma((5,)),
+            pltpu.VMEM((3, half, ff), F32), dma((4,)),
         ],
         compiler_params=pltpu.CompilerParams(
             collective_id=0, has_side_effects=True, vmem_limit_bytes=VMEM_LIMIT
@@ -372,7 +415,7 @@
             pl.BlockSpec((count // steps, width), lambda i: (i, 0)),
             part_out, part_out, part_out,
         ),
-        compiler_params=pltpu.CompilerParams(vmem_limit_bytes=32000000),
+        compiler_params=pltpu.CompilerParams(vmem_limit_bytes=VMEM_LIMIT),
         name="finish",
     )(hot, came_back, gate_gradient, up_gradient, down_gradient))
 

time: 97.1 us -> 90.1 us (0.928)
  local copies, waits for them, and re-layouts: 5.23 us -> 0 us
  Pallas kernels: 90.9 us -> 89.3 us
    unnamed x10 -> x0, local copies, waits for them, and re-layouts: 5.23 us -> none
    pallas_call x1, Pallas kernels: 87.9 us -> 84.8 us  [on_device(): pl.pallas_call(functools.partial(kernel, planes, experts, slots, (groups...]
    pallas_call x1, Pallas kernels: 3.04 us -> 4.52 us  [on_device(): pl.pallas_call(finish, grid=(steps,), out_shape=(jax.ShapeDtypeStruct((co...]
where the time goes in v3:
time: 90.1 us; the launch traced here: 90 us
  Pallas kernels  89.3 us (99%)
    pallas_call x1, Pallas kernels, on_device(): pl.pallas_call(functools.partial(kernel, planes, experts, slots, (groups...  84.8 us
    pallas_call x1, Pallas kernels, on_device(): pl.pallas_call(finish, grid=(steps,), out_shape=(jax.ShapeDtypeStruct((co...  4.52 us

profile of v3, /device:TPU:0, one launch (start us, length us, event | category | flops | bytes accessed | tf_op | source)
XLA Modules:
  0.0 90.0 jit_solution(5559549125590348299)
XLA Ops:
  0.6 84.8 %routed_layer.1 = (bf16[64,2048]{1,0:T(8,128)(2,1)}, bf16[64,768]{1,0:T(8,128)(2,1)}, f32[256,768]{1,0:T(8,128)}, f32[256,768]{1,0:T(8,128)}, f32[256,768]{1,0:T(8,128)}) custom-call(s32[1,4,1,16]{3,2,1,0:T(1,128)} %index.1, s32[1,4]{1,0:T(1,128)} %bitcast.7, f32[1,4,1,16]{3,2,1,0:T(1,128)} %gate.1, bf16[768,2048]{1,0:T(8,128)(2,1)} %tokens.1, ...), custom_call_target="tpu_custom_call" | custom-call | tf_op jit(solution)/shard_map/routed_layer/pallas_call | solution.py:352
  85.4 4.5 %finish.1 = (bf16[768,2048]{1,0:T(8,128)(2,1)}, f32[256,1,768]{2,1,0:T(1,128)}, f32[256,1,768]{2,1,0:T(1,128)}, f32[256,1,768]{2,1,0:T(1,128)}) custom-call(bf16[64,768]{1,0:T(8,128)(2,1)} %get-tuple-element.9.hot, bf16[64,2048]{1,0:T(8,128)(2,1)} %get-tuple-element.10.cb, f32[256,768]{1,0:T(8,128)} %get-tuple-element.11.gg, ...), custom_call_target="tpu_custom_call" | custom-call | tf_op jit(solution)/shard_map/finish/pallas_call | solution.py:405

commit v4 on v3

--- a/solution.py
+++ b/solution.py
@@ -299,23 +299,27 @@
             + dot(GU[1, group_rows(z), :], weight(1), NT)
         ).astype(BF16)
         sources(RG, CB, 3, z)
+        for i in range(2):
+            remote(
+                GU.at[i, group_rows(z)], GUX.at[i, group_rows(z)],
+                x_send.at[3 + i], x_recv.at[3 + i], sibling,
+            )
 
     along([GU.at[0], GU.at[1]], 1, row_grad)
-    x_gate = remote(GU.at[0], GUX.at[0], x_send.at[3], x_recv.at[3], sibling)
-    x_up = remote(GU.at[1], GUX.at[1], x_send.at[4], x_recv.at[4], sibling)
+    own_sums = [dot(R[:, keep], GU[i], TN) for i in range(2)]
     x_rows.wait_recv()
-    x_gate.wait_recv()
-    GRADS[0] = (dot(R[:, keep], GU[0], TN) + dot(RX[...], GUX[0], TN)) * factor
-    put(0, GRADS.at[0], gg_out)
-    x_up.wait_recv()
-    GRADS[1] = (dot(R[:, keep], GU[1], TN) + dot(RX[...], GUX[1], TN)) * factor
-    put(1, GRADS.at[1], ug_out)
+    for i, out in enumerate((gg_out, ug_out)):
+        take(x_recv.at[3 + i], GUX.at[i])
+        GRADS[i] = (own_sums[i] + dot(RX[...], GUX[i], TN)) * factor
+        put(i, GRADS.at[i], out)
     for k in order + [0]:
         arrived(3, k)
     put(3, CB, cb_out)
 
-    for c in sent_w + [x_rows, x_hidden, x_grad, x_gate, x_up]:
+    for c in sent_w + [x_rows, x_hidden, x_grad]:
         c.wait_send()
+    for i in range(2):
+        take(x_send.at[3 + i], GUX.at[i])
     for i in range(4):
         take(a_send.at[i], R.at[pl.ds(0, (peers - 1) * slots)])
     for i in range(3):

time: 90.1 us -> 90.1 us (level)
  no operation moved by 1% of the time
where the time goes in v4:
time: 90.1 us; the launch traced here: 90 us
  Pallas kernels  89.3 us (99%)
    pallas_call x1, Pallas kernels, on_device(): pl.pallas_call(functools.partial(kernel, planes, experts, slots, (groups...  84.8 us
    pallas_call x1, Pallas kernels, on_device(): pl.pallas_call(finish, grid=(steps,), out_shape=(jax.ShapeDtypeStruct((co...  4.52 us

profile of v4, /device:TPU:0, one launch (start us, length us, event | category | flops | bytes accessed | tf_op | source)
XLA Modules:
  0.0 90.0 jit_solution(16181449743505936331)
XLA Ops:
  0.6 84.8 %routed_layer.1 = (bf16[64,2048]{1,0:T(8,128)(2,1)}, bf16[64,768]{1,0:T(8,128)(2,1)}, f32[256,768]{1,0:T(8,128)}, f32[256,768]{1,0:T(8,128)}, f32[256,768]{1,0:T(8,128)}) custom-call(s32[1,4,1,16]{3,2,1,0:T(1,128)} %index.1, s32[1,4]{1,0:T(1,128)} %bitcast.7, f32[1,4,1,16]{3,2,1,0:T(1,128)} %gate.1, bf16[768,2048]{1,0:T(8,128)(2,1)} %tokens.1, ...), custom_call_target="tpu_custom_call" | custom-call | tf_op jit(solution)/shard_map/routed_layer/pallas_call | solution.py:356
  85.4 4.5 %finish.1 = (bf16[768,2048]{1,0:T(8,128)(2,1)}, f32[256,1,768]{2,1,0:T(1,128)}, f32[256,1,768]{2,1,0:T(1,128)}, f32[256,1,768]{2,1,0:T(1,128)}) custom-call(bf16[64,768]{1,0:T(8,128)(2,1)} %get-tuple-element.9.hot, bf16[64,2048]{1,0:T(8,128)(2,1)} %get-tuple-element.10.cb, f32[256,768]{1,0:T(8,128)} %get-tuple-element.11.gg, ...), custom_call_target="tpu_custom_call" | custom-call | tf_op jit(solution)/shard_map/finish/pallas_call | solution.py:409
